TPU v7x, 32 devices: a whole 2x2x4 slice. The times are simulated.
32 devices in a mesh: dp: 8 (over z, x), tensor: 4 (over y, core).
Axes of the slice: x: 2, y: 2, z: 4, core: 2. Of those that a mesh axis runs over, the one named last changes fastest.
Arguments:
- features: bfloat16 [3072, 8192], P('dp', 'tensor'), may hold values from -6 to 6
- key_value_weight: bfloat16 [8192, 2048], P('tensor'), may hold values from -0.0625 to 0.0625
- adapter_down_weight: bfloat16 [32, 64, 8192], P('dp', None, 'tensor'), may hold values from -0.0625 to 0.0625
- adapter_up_weight: bfloat16 [32, 64, 2048], P('dp', None, 'tensor'), may hold values from -0.75 to 0.75
- token_adapter_index: int32 [3072], P('dp'), may hold values from 0 to 31, as said below
- adapter_position: int32 [32], replicated, may hold values from 0 to 31, as said below
- output_gradient: bfloat16 [3072, 2048], P('dp', 'tensor'), may hold values from -6 to 6
Outputs:
- key_value_output: bfloat16 [3072, 2048], P('dp', 'tensor')
- feature_gradient: bfloat16 [3072, 8192], P('dp', 'tensor')
- down_gradient: float32 [32, 64, 8192], P('dp', None, 'tensor')
- up_gradient: float32 [32, 64, 2048], P('dp', None, 'tensor')
Inputs may be any that keep to these rules, and one draw needn't show every extreme that they name: `token_adapter_index`: within each aligned block of 384 tokens (those of one index of dp) the ids do not fall. Call slot // 4 the storing index of an adapter; in each block at most 144 tokens have adapters of one storing index. In every draw one storing index, the same for all blocks, gets exactly 144 tokens from every block, and in every block another storing index, which varies from block to block, gets exactly 144 tokens as well. A permutation: adapter a is stored at slot adapter_position[a].
All inputs are finite; a program needn't handle non-finite values.
Results may differ from a plain program's by a relative error of at most 0.0054.
Values may be sent and summed in bfloat16 or wider, within the bound.
A program may use at most 64 MiB of HBM per device.

v0:
```python
import jax
import jax.numpy as jnp
from jax import lax
from jax.sharding import PartitionSpec as P

adapter_scale = 2.0


def contract_trailing(left, right):
    return lax.dot_general(
        left, right, (((1,), (1,)), ((), ())), preferred_element_type=jnp.float32
    )


def contract_leading(left, right):
    return lax.dot_general(
        left, right, (((0,), (0,)), ((), ())), preferred_element_type=jnp.float32
    )


def body(
    features,
    key_value_weight,
    adapter_down_weight,
    adapter_up_weight,
    token_adapter_index,
    adapter_position,
    output_gradient,
):
    token_groups = lax.axis_size("dp")
    tok_rows, width_local = features.shape
    output_local = output_gradient.shape[1]
    adapter_local_count, rank_axis_size, unused_value = adapter_down_weight.shape
    row_capacity = 3 * tok_rows // token_groups
    holding_rows = token_groups * row_capacity
    adapter_ids = jnp.arange(adapter_position.shape[0], dtype=jnp.int32)
    matches = token_adapter_index[:, None] == adapter_ids[None, :]
    slot_tok = jnp.sum(jnp.where(matches, adapter_position[None, :], 0), axis=1)
    owner_of = slot_tok // adapter_local_count
    local_id = slot_tok % adapter_local_count
    owner_hits = (owner_of[:, None] == jnp.arange(token_groups, dtype=jnp.int32)[None, :]).astype(
        jnp.int32
    )
    rank_in = jnp.sum((jnp.cumsum(owner_hits, axis=0) - 1) * owner_hits, axis=1)
    target_slot = owner_of * row_capacity + rank_in

    def to_buffer(source):
        filled = (
            jnp.zeros((holding_rows, source.shape[1]), source.dtype).at[target_slot].set(source)
        )
        return filled.reshape(token_groups, row_capacity, source.shape[1])

    id_buffer = (
        jnp.full((holding_rows,), -1.0, jnp.bfloat16)
        .at[target_slot]
        .set(local_id.astype(jnp.bfloat16))
    )
    id_buffer = id_buffer.reshape(token_groups, row_capacity)
    lane_ids = (
        jnp.arange(adapter_local_count * rank_axis_size, dtype=jnp.int32) // rank_axis_size
    ).astype(jnp.bfloat16)
    down_matrix = adapter_down_weight.reshape(adapter_local_count * rank_axis_size, width_local)
    up_matrix = adapter_up_weight.reshape(adapter_local_count * rank_axis_size, output_local)

    def compact_rows(values, slot_selector):
        return jnp.sum(
            (values * slot_selector).reshape(holding_rows, adapter_local_count, rank_axis_size),
            axis=1,
        )

    def expand(values, slot_selector):
        return (
            jnp.tile(values, (1, adapter_local_count)).astype(jnp.float32) * slot_selector
        ).astype(jnp.bfloat16)

    columns = key_value_weight
    gradient_frozen = contract_trailing(
        lax.all_gather(output_gradient, "tensor", axis=1, tiled=True), columns
    )
    rows_recv, ids_recv = (
        lax.all_to_all(to_buffer(features), "dp", split_axis=0, concat_axis=0, tiled=True),
        lax.all_to_all(id_buffer, "dp", split_axis=0, concat_axis=0, tiled=True),
    )
    rows_in = rows_recv.reshape(holding_rows, width_local)
    slot_selector = (ids_recv.reshape(holding_rows)[:, None] == lane_ids[None, :]).astype(
        jnp.float32
    )
    down_part = compact_rows(contract_trailing(rows_in, down_matrix), slot_selector)
    down_total = lax.psum(down_part, "tensor")
    down_gathered = expand(down_total.astype(jnp.bfloat16), slot_selector)
    adapter_row_block = (
        adapter_scale * jnp.dot(down_gathered, up_matrix, preferred_element_type=jnp.float32)
    ).astype(jnp.bfloat16)
    adapter_backward = lax.all_to_all(
        adapter_row_block.reshape(token_groups, row_capacity, output_local),
        "dp",
        split_axis=0,
        concat_axis=0,
        tiled=True,
    )
    grads_recv = lax.all_to_all(
        to_buffer(output_gradient), "dp", split_axis=0, concat_axis=0, tiled=True
    )
    incoming_gradients = grads_recv.reshape(holding_rows, output_local)
    up_partial = compact_rows(
        adapter_scale * contract_trailing(incoming_gradients, up_matrix), slot_selector
    )
    up_combined = lax.psum(up_partial, "tensor")
    up_wide = expand(up_combined.astype(jnp.bfloat16), slot_selector)
    input_row_block = jnp.dot(up_wide, down_matrix, preferred_element_type=jnp.float32).astype(
        jnp.bfloat16
    )
    input_back = lax.all_to_all(
        input_row_block.reshape(token_groups, row_capacity, width_local),
        "dp",
        split_axis=0,
        concat_axis=0,
        tiled=True,
    )
    down_gradient = contract_leading(up_wide, rows_in).reshape(
        adapter_local_count, rank_axis_size, width_local
    )
    up_gradient = (adapter_scale * contract_leading(down_gathered, incoming_gradients)).reshape(
        adapter_local_count, rank_axis_size, output_local
    )
    adapter_token_rows = adapter_backward.reshape(holding_rows, output_local)[target_slot]
    input_tok = input_back.reshape(holding_rows, width_local)[target_slot]
    columns = key_value_weight
    key_value_frozen = lax.psum_scatter(
        contract_leading(columns, features.T), "tensor", scatter_dimension=0, tiled=True
    ).T
    key_value_output = (key_value_frozen + adapter_token_rows.astype(jnp.float32)).astype(
        jnp.bfloat16
    )
    feature_gradient = (gradient_frozen + input_tok.astype(jnp.float32)).astype(jnp.bfloat16)
    return (key_value_output, feature_gradient, down_gradient, up_gradient)


def solution(mesh):
    placed = (
        P("dp", "tensor"),
        P("tensor", None),
        P("dp", None, "tensor"),
        P("dp", None, "tensor"),
        P("dp"),
        P(),
        P("dp", "tensor"),
    )
    return jax.shard_map(
        body,
        mesh=mesh,
        in_specs=placed,
        out_specs=(
            P("dp", "tensor"),
            P("dp", "tensor"),
            P("dp", None, "tensor"),
            P("dp", None, "tensor"),
        ),
        check_vma=False,
    )
```

profile of v0, /device:TPU:0, one launch (start us, length us, event | category | flops | bytes accessed | tf_op | source)
XLA Modules:
  0.0 354.7 jit_solution(9046061355832921624)
XLA Ops:
  7.2 0.0 copy-start
  7.2 0.9 select_reduce_fusion
  8.1 0.9 reduce-window.6
  9.0 0.2 slice_reduce_fusion
  9.2 0.1 fusion.16
  9.3 0.0 copy-start.4
  9.4 3.0 scatter_custom_fusion
  12.3 0.7 all_to_all.24
  13.0 7.3 %all-to-all-start = ((bf16[8,1,144]{2,1,0:T(2,128)(2,1)}), bf16[8,1,144]{2,1,0:T(2,128)(2,1)S(1)}, u32[]{:S(2)}, u32[]{:S(2)}) async-start(bf16[8,1,144]{2,1,0:T(2,128)(2,1)} %all_to_all.24), calls=%async_computation.1 | async-start | bytes 16384 | tf_op jit(solution)/shard_map/all_to_all | solution.py:82
  20.3 3.6 %scatter_custom_fusion.2 = bf16[1152,512]{1,0:T(8,128)(2,1)} fusion(s32[384]{0:T(512)S(1)} %fusion.27, bf16[384,512]{1,0:T(8,128)(2,1)} %param.13, bf16[]{:T(256)} %constant.71.clone.1), kind=kCustom, calls=%fused_computation.25 | custom fusion | bytes 1180160 | tf_op jit(solution)/shard_map/scatter | solution.py:49
  23.9 3.0 all-to-all-done
  26.8 3.6 %all-to-all-start.3 = ((bf16[8,144,512]{2,1,0:T(8,128)(2,1)}), bf16[8,144,512]{2,1,0:T(8,128)(2,1)S(1)}, u32[]{:S(2)}, u32[]{:S(2)}) async-start(bf16[8,144,512]{2,1,0:T(8,128)(2,1)} %bitcast.11), calls=%async_computation.4 | async-start | bytes 2359296 | tf_op jit(solution)/shard_map/all_to_all | solution.py:101
  30.4 0.0 copy-done.4
  30.4 6.7 %scatter_custom_fusion.1 = bf16[1152,2048]{1,0:T(8,128)(2,1)} fusion(s32[384]{0:T(512)S(1)} %fusion.27, bf16[384,2048]{1,0:T(8,128)(2,1)} %param.7, bf16[]{:T(256)} %constant.71.clone.1), kind=kCustom, calls=%fused_computation.13 | custom fusion | bytes 4719104 | tf_op jit(solution)/shard_map/scatter | solution.py:49
  37.1 21.0 %all-to-all-done.3 = bf16[8,144,512]{2,1,0:T(8,128)(2,1)S(1)} async-done(((bf16[8,144,512]{2,1,0:T(8,128)(2,1)}), bf16[8,144,512]{2,1,0:T(8,128)(2,1)S(1)}, u32[]{:S(2)}, u32[]{:S(2)}) %all-to-all-start.3) | async-done | bytes 1179680 | tf_op jit(solution)/shard_map/all_to_all | solution.py:101
  58.1 4.8 %all-to-all-start.1 = ((bf16[8,144,2048]{2,1,0:T(8,128)(2,1)}), bf16[8,144,2048]{2,1,0:T(8,128)(2,1)}, u32[]{:S(2)}, u32[]{:S(2)}) async-start(bf16[8,144,2048]{2,1,0:T(8,128)(2,1)} %bitcast.74), calls=%async_computation.2 | async-start | bytes 9437184 | tf_op jit(solution)/shard_map/all_to_all | solution.py:81
  62.9 0.0 copy-start.5
  62.9 0.6 fusion.20
  63.5 0.1 eq.81
  63.6 0.0 copy-start.2
  63.6 1.5 fusion.2
  65.1 0.8 reduce_sum.48
  65.9 100.3 %all-to-all-done.1 = bf16[8,144,2048]{2,1,0:T(8,128)(2,1)} async-done(((bf16[8,144,2048]{2,1,0:T(8,128)(2,1)}), bf16[8,144,2048]{2,1,0:T(8,128)(2,1)}, u32[]{:S(2)}, u32[]{:S(2)}) %all-to-all-start.1) | async-done | bytes 4718624 | tf_op jit(solution)/shard_map/all_to_all | solution.py:81
  166.3 0.0 copy-done
  166.3 0.0 copy-done.5
  166.3 0.0 copy-done.2
  166.3 3.9 %convolution_select_fusion = f32[1152,256]{0,1:T(8,128)S(1)} fusion(bf16[1152,2048]{1,0:T(8,128)(2,1)} %bitcast.5, bf16[256,2048]{1,0:T(8,128)(2,1)S(1)} %bitcast.73, bf16[1152]{0:T(1024)(128)(2,1)S(1)} %eq.81, bf16[256]{0:T(256)(128)(2,1)S(1)} %fusion.28), kind=kOutput, calls=%fused_computation.12 | convolution fusion | flops 1208549376 | bytes 6949632 | tf_op jit(solution)/shard_map/dot_general | solution.py:10
  170.2 0.8 reduce_sum.47
  171.0 17.6 %all-reduce.2 = (bf16[1152,64]{0,1:T(8,128)(2,1)S(1)}, bf16[1152,64]{0,1:T(8,128)(2,1)S(1)}) all-reduce(f32[1152,64]{0,1:T(8,128)} %reduce_sum.47, f32[1152,64]{0,1:T(8,128)} %reduce_sum.48), channel_id=1, replica_groups=mesh['dp'=8,'tensor'=4] {'tensor'}, use_global_device_ids=true, to_apply=%region_8.9 | all-reduce | flops 147456 | bytes 884736 | tf_op jit(solution)/shard_map/psum | solution.py:89
  188.6 0.0 copy-start.1
  188.6 2.6 fusion.1
  191.2 0.0 copy-done.1
  191.2 4.0 %all-to-all-start.2 = ((bf16[8,144,512]{2,1,0:T(8,128)(2,1)}), bf16[8,144,512]{2,1,0:T(8,128)(2,1)S(1)}, u32[]{:S(2)}, u32[]{:S(2)}) async-start(bf16[8,144,512]{2,1,0:T(8,128)(2,1)} %bitcast.80), calls=%async_computation.3 | async-start | bytes 2359296 | tf_op jit(solution)/shard_map/all_to_all | solution.py:94
  195.3 0.0 reduce-scatter.2.cloned.1.call-start
  195.3 10.0 %fusion.31 = f32[2048,384]{1,0:T(8,128)} fusion(bf16[2048,2048]{1,0:T(8,128)(2,1)} %param.8, bf16[384,2048]{1,0:T(8,128)(2,1)} %param.7), kind=kOutput, calls=%fused_computation.79 | convolution fusion | flops 3221225472 | bytes 13107200 | tf_op jit(solution)/shard_map/dot_general | solution.py:16
  205.3 0.0 reduce-scatter.2.cloned.1.call-update
  205.3 4.4 %bitcast_convert_fusion = bf16[1152,2048]{1,0:T(8,128)(2,1)} fusion(bf16[4,64,2048]{2,1,0:T(8,128)(2,1)S(1)} %copy-done, bf16[1152,64]{0,1:T(8,128)(2,1)S(1)} %get-tuple-element.21, bf16[4,64]{1,0:T(4,128)(2,1)} %fusion.20, bf16[1152]{0:T(1024)(128)(2,1)} %copy-done.2), kind=kOutput, calls=%fused_computation.5 | convolution fusion | flops 1211498496 | bytes 5917440 | tf_op jit(solution)/shard_map/dot_general | solution.py:110
  209.8 13.9 %all-to-all-done.2 = bf16[8,144,512]{2,1,0:T(8,128)(2,1)S(1)} async-done(((bf16[8,144,512]{2,1,0:T(8,128)(2,1)}), bf16[8,144,512]{2,1,0:T(8,128)(2,1)S(1)}, u32[]{:S(2)}, u32[]{:S(2)}) %all-to-all-start.2) | async-done | bytes 1179680 | tf_op jit(solution)/shard_map/all_to_all | solution.py:94
  223.7 4.6 %all-to-all-start.4 = ((bf16[8,144,2048]{2,1,0:T(8,128)(2,1)}), bf16[8,144,2048]{2,1,0:T(8,128)(2,1)}, u32[]{:S(2)}, u32[]{:S(2)}) async-start(bf16[8,144,2048]{2,1,0:T(8,128)(2,1)} %bitcast.76), calls=%async_computation.5 | async-start | bytes 9437184 | tf_op jit(solution)/shard_map/all_to_all | solution.py:113
  228.3 0.3 all-gather.2.cloned.1.call-start
  228.6 0.5 all-gather.2.cloned.1.call-update
  229.1 1.3 pad_clamp_fusion
  230.4 0.9 fusion.7
  231.3 1.1 fusion.5
  232.4 1.3 convolution_multiply_fusion.1
  233.7 0.0 copy-start.3
  233.7 5.2 %fusion.32 = f32[4,64,2048]{2,1,0:T(8,128)} fusion(bf16[4,64,1152]{2,1,0:T(8,128)(2,1)S(1)} %bitcast.83, bf16[1152,2048,1]{1,0,2:T(8,128)(2,1)} %bitcast.21), kind=kOutput, calls=%fused_computation.80 | convolution fusion | flops 1207959552 | bytes 7405568 | tf_op jit(solution)/shard_map/dot_general | solution.py:16
  238.9 0.0 copy-done.3
  238.9 2.1 gather_fusion
  241.0 0.2 copy.19
  241.2 3.0 reduce-scatter.2.cloned.1.call-done
  244.2 1.2 fusion.8
  245.5 0.9 copy.20
  246.4 85.7 %all-to-all-done.4 = bf16[8,144,2048]{2,1,0:T(8,128)(2,1)} async-done(((bf16[8,144,2048]{2,1,0:T(8,128)(2,1)}), bf16[8,144,2048]{2,1,0:T(8,128)(2,1)}, u32[]{:S(2)}, u32[]{:S(2)}) %all-to-all-start.4) | async-done | bytes 4718624 | tf_op jit(solution)/shard_map/all_to_all | solution.py:113
  332.1 7.3 %gather_fusion.1 = bf16[384,2048]{1,0:T(8,128)(2,1)S(1)} fusion(bf16[1152,2048]{1,0:T(8,128)(2,1)} %bitcast.17, s32[1024]{0:T(1024)S(1)} %copy-done.3), kind=kCustom, calls=%fused_computation.1 | custom fusion | bytes 3147264 | tf_op jit(solution)/shard_map/gather | solution.py:127
  339.4 0.0 all-gather.2.cloned.1.call-done
  339.4 8.5 %add_convert_fusion = bf16[384,2048]{1,0:T(8,128)(2,1)} fusion(bf16[384,2048]{1,0:T(8,128)(2,1)S(1)} %gather_fusion.1, bf16[384,2048]{1,0:T(8,128)(2,1)} %all-gather.2.cloned.1.call-done, bf16[2048,2048]{1,0:T(8,128)(2,1)} %param.8), kind=kOutput, calls=%fused_computation.8 | convolution fusion | flops 3223584768 | bytes 13107200 | tf_op jit(solution)/shard_map/dot_general | solution.py:10
  (7 shorter events, 0.1 us)
Async XLA Ops:
  7.2 159.1 %copy-start = (bf16[4,64,2048]{2,1,0:T(8,128)(2,1)S(1)}, bf16[4,64,2048]{2,1,0:T(8,128)(2,1)}, u32[]{:S(2)}) copy-start(bf16[4,64,2048]{2,1,0:T(8,128)(2,1)} %param.9) | copy-start | bytes 3145732
  9.3 21.1 %copy-start.4 = (s32[384]{0:T(512)}, s32[384]{0:T(512)S(1)}, u32[]{:S(2)}) copy-start(s32[384]{0:T(512)S(1)} %fusion.27) | copy-start | bytes 4612
  13.0 13.8 %all-to-all-start = ((bf16[8,1,144]{2,1,0:T(2,128)(2,1)}), bf16[8,1,144]{2,1,0:T(2,128)(2,1)S(1)}, u32[]{:S(2)}, u32[]{:S(2)}) async-start(bf16[8,1,144]{2,1,0:T(2,128)(2,1)} %all_to_all.24), calls=%async_computation.1 | async-start | bytes 16384 | tf_op jit(solution)/shard_map/all_to_all | solution.py:82
  26.8 31.3 %all-to-all-start.3 = ((bf16[8,144,512]{2,1,0:T(8,128)(2,1)}), bf16[8,144,512]{2,1,0:T(8,128)(2,1)S(1)}, u32[]{:S(2)}, u32[]{:S(2)}) async-start(bf16[8,144,512]{2,1,0:T(8,128)(2,1)} %bitcast.11), calls=%async_computation.4 | async-start | bytes 2359296 | tf_op jit(solution)/shard_map/all_to_all | solution.py:101
  58.1 108.2 %all-to-all-start.1 = ((bf16[8,144,2048]{2,1,0:T(8,128)(2,1)}), bf16[8,144,2048]{2,1,0:T(8,128)(2,1)}, u32[]{:S(2)}, u32[]{:S(2)}) async-start(bf16[8,144,2048]{2,1,0:T(8,128)(2,1)} %bitcast.74), calls=%async_computation.2 | async-start | bytes 9437184 | tf_op jit(solution)/shard_map/all_to_all | solution.py:81
  62.9 103.4 %copy-start.5 = (bf16[256]{0:T(256)(128)(2,1)}, bf16[256]{0:T(256)(128)(2,1)S(1)}, u32[]{:S(2)}) copy-start(bf16[256]{0:T(256)(128)(2,1)S(1)} %fusion.28) | copy-start | bytes 1540
  63.6 102.7 %copy-start.2 = (bf16[1152]{0:T(1024)(128)(2,1)}, bf16[1152]{0:T(1024)(128)(2,1)S(1)}, u32[]{:S(2)}) copy-start(bf16[1152]{0:T(1024)(128)(2,1)S(1)} %eq.81) | copy-start | bytes 6916
  188.6 2.6 copy-start.1
  191.2 32.5 %all-to-all-start.2 = ((bf16[8,144,512]{2,1,0:T(8,128)(2,1)}), bf16[8,144,512]{2,1,0:T(8,128)(2,1)S(1)}, u32[]{:S(2)}, u32[]{:S(2)}) async-start(bf16[8,144,512]{2,1,0:T(8,128)(2,1)} %bitcast.80), calls=%async_computation.3 | async-start | bytes 2359296 | tf_op jit(solution)/shard_map/all_to_all | solution.py:94
  195.3 49.0 %reduce-scatter.2.cloned.1.call-start = ((), (), s32[]{:S(2)}) async-start(), calls=%async_computation.6 | async-start | bytes 3932160 | tf_op jit(solution)/shard_map/reduce_scatter | solution.py:129
  223.7 108.3 %all-to-all-start.4 = ((bf16[8,144,2048]{2,1,0:T(8,128)(2,1)}), bf16[8,144,2048]{2,1,0:T(8,128)(2,1)}, u32[]{:S(2)}, u32[]{:S(2)}) async-start(bf16[8,144,2048]{2,1,0:T(8,128)(2,1)} %bitcast.76), calls=%async_computation.5 | async-start | bytes 9437184 | tf_op jit(solution)/shard_map/all_to_all | solution.py:113
  228.3 111.1 %all-gather.2.cloned.1.call-start = ((), (), s32[]{:S(2)}) async-start(), calls=%async_computation.7 | async-start | bytes 1966080 | tf_op jit(solution)/shard_map/all_gather | solution.py:78
  233.7 5.3 %copy-start.3 = (s32[1024]{0:T(1024)S(1)}, s32[1024]{0:T(1024)}, u32[]{:S(2)}) copy-start(s32[1024]{0:T(1024)} %pad_clamp_fusion) | copy-start | bytes 12292
Sparse Core Ops, SparseCore 0:
  205.5 38.7 reduce-scatter.1
  245.8 19.6 all-gather.1
where the time goes:
time: 356 us; the launch traced here: 355 us
  waiting for transfers between devices  227 us (64%)
  matrix products  37.5 us (11%)
  local copies, waits for them, and re-layouts  24.8 us (7%)
  starting transfers between devices  24.6 us (7%)
  blocking collectives  17.6 us (5%)
  between operations  14.2 us (4%)
  other arithmetic  8.58 us (2%)
    all_to_all x1, waiting for transfers between devices, body(): lax.all_to_all(to_buffer(features), 'dp', split_axis=0, concat_axis=0, ti...  100 us
    all_to_all x1, waiting for transfers between devices, body(): lax.all_to_all(input_row_block.reshape(token_groups, row_capacity, width_...  85.7 us
    all_to_all x1, waiting for transfers between devices, body(): lax.all_to_all(to_buffer(output_gradient), 'dp', split_axis=0, concat_axi...  21 us
    psum x1, blocking collectives, body(): down_total = lax.psum(down_part, 'tensor')  17.6 us
    dot_general x3, matrix products, contract_leading(): lax.dot_general(left, right, (((0,), (0,)), ((), ())), preferred_element_...  16.6 us
    all_to_all x1, waiting for transfers between devices, body(): lax.all_to_all(adapter_row_block.reshape(token_groups, row_capacity, outp...  13.9 us
    dot_general x3, matrix products, contract_trailing(): lax.dot_general(left, right, (((1,), (1,)), ((), ())), preferred_element_...  13.8 us
    scatter x2, local copies, waits for them, and re-layouts, to_buffer(): jnp.zeros((holding_rows, source.shape[1]), source.dtype).at[target_slot]  10.3 us
  transfers between devices with their start and end apart: 7, of which 6 were waited for; matrix products, arithmetic and copies ran while one was open for 14% of the time, Pallas kernels for 0%

commit v1 on v0

--- a/solution.py
+++ b/solution.py
@@ -2,8 +2,26 @@
 import jax.numpy as jnp
 from jax import lax
 from jax.sharding import PartitionSpec as P
+from jax.lax import axis_index, ppermute, psum
 
 adapter_scale = 2.0
+
+
+def produce_threads_in(work_x, array_dim, obj):
+    top = work_x.shape
+    return jnp.moveaxis(
+        work_x.reshape(*top[:array_dim], obj, top[array_dim] // obj, *top[array_dim + 1 :]),
+        array_dim,
+        0,
+    )
+
+
+def widths_watch(my_data, join_dim):
+    my_data = jnp.moveaxis(my_data, 0, join_dim)
+    response = my_data.shape
+    return my_data.reshape(
+        *response[:join_dim], response[join_dim] * response[join_dim + 1], *response[join_dim + 2 :]
+    )
 
 
 def contract_trailing(left, right):
@@ -91,12 +109,24 @@
     adapter_row_block = (
         adapter_scale * jnp.dot(down_gathered, up_matrix, preferred_element_type=jnp.float32)
     ).astype(jnp.bfloat16)
-    adapter_backward = lax.all_to_all(
-        adapter_row_block.reshape(token_groups, row_capacity, output_local),
-        "dp",
-        split_axis=0,
-        concat_axis=0,
-        tiled=True,
+
+    def _group_pieces_all(incoming_x, across, vector, buf):
+        parts_out, met_up = (psum(1, across), axis_index(across))
+        mat_out = produce_threads_in(incoming_x, vector, parts_out)
+        y1 = mat_out
+        u = 1
+        while u < parts_out:
+            later, new = ((met_up + u) % parts_out, (met_up - u) % parts_out)
+            all_values = lax.dynamic_index_in_dim(mat_out, later, 0)
+            u1 = ppermute(
+                all_values, across, tuple(((c, (c + u) % parts_out) for c in range(parts_out)))
+            )
+            y1 = lax.dynamic_update_slice_in_dim(y1, u1, new, axis=0)
+            u = u + 1
+        return widths_watch(y1, buf)
+
+    adapter_backward = _group_pieces_all(
+        adapter_row_block.reshape(token_groups, row_capacity, output_local), "dp", 0, 0
     )
     grads_recv = lax.all_to_all(
         to_buffer(output_gradient), "dp", split_axis=0, concat_axis=0, tiled=True

time: 356 us -> 360 us (1.011)
  starting transfers between devices: 24.6 us -> 54.2 us
  waiting for transfers between devices: 227 us -> 204 us
    ppermute x0 -> x7, waiting for transfers between devices: none -> 89.5 us  [_group_pieces_all(): ppermute(all_values, across, tuple(((c, (c + u) % parts_out) for c in ran...]
    all_to_all x1, waiting for transfers between devices: 85.7 us -> 0.01 us  [body(): lax.all_to_all(input_row_block.reshape(token_groups, row_capacity, width_...]
    ppermute x0 -> x7, starting transfers between devices: none -> 33.8 us  [_group_pieces_all(): ppermute(all_values, across, tuple(((c, (c + u) % parts_out) for c in ran...]
    all_to_all x1 -> x0, waiting for transfers between devices: 13.9 us -> none  [body(): lax.all_to_all(adapter_row_block.reshape(token_groups, row_capacity, outp...]
    all_to_all x1, waiting for transfers between devices: 100 us -> 90.2 us  [body(): lax.all_to_all(to_buffer(features), 'dp', split_axis=0, concat_axis=0, ti...]
    all_to_all x1 -> x0, starting transfers between devices: 4.04 us -> none  [body(): lax.all_to_all(adapter_row_block.reshape(token_groups, row_capacity, outp...]
  transfers between devices with their start and end apart: 7 -> 13, of which waited for: 6 -> 7; matrix products, arithmetic and copies ran while one was open for 14% -> 15% of each run, Pallas kernels for 0% -> 0%
where the time goes in v1:
time: 360 us; the launch traced here: 359 us
  waiting for transfers between devices  204 us (57%)
  starting transfers between devices  54.2 us (15%)
  matrix products  36.5 us (10%)
  local copies, waits for them, and re-layouts  25 us (7%)
  blocking collectives  18.1 us (5%)
  between operations  14.6 us (4%)
  other arithmetic  6.29 us (2%)
    all_to_all x1, waiting for transfers between devices, body(): lax.all_to_all(to_buffer(features), 'dp', split_axis=0, concat_axis=0, ti...  90.2 us
    ppermute x7, waiting for transfers between devices, _group_pieces_all(): ppermute(all_values, across, tuple(((c, (c + u) % parts_out) for c in ran...  89.5 us
    ppermute x7, starting transfers between devices, _group_pieces_all(): ppermute(all_values, across, tuple(((c, (c + u) % parts_out) for c in ran...  33.8 us
    all_to_all x1, waiting for transfers between devices, body(): lax.all_to_all(to_buffer(output_gradient), 'dp', split_axis=0, concat_axi...  21 us
    psum x1, blocking collectives, body(): down_total = lax.psum(down_part, 'tensor')  18.1 us
    dot_general x3, matrix products, contract_leading(): lax.dot_general(left, right, (((0,), (0,)), ((), ())), preferred_element_...  16.5 us
    dot_general x3, matrix products, contract_trailing(): lax.dot_general(left, right, (((1,), (1,)), ((), ())), preferred_element_...  13.8 us
    scatter x2, local copies, waits for them, and re-layouts, to_buffer(): jnp.zeros((holding_rows, source.shape[1]), source.dtype).at[target_slot]  10.3 us
  transfers between devices with their start and end apart: 13, of which 7 were waited for; matrix products, arithmetic and copies ran while one was open for 15% of the time, Pallas kernels for 0%

profile of v1, /device:TPU:0, one launch (start us, length us, event | category | flops | bytes accessed | tf_op | source)
XLA Modules:
  0.0 359.1 jit_solution(17974815096960726965)
XLA Ops:
  7.2 0.0 copy-start
  7.2 0.9 select_reduce_fusion
  8.1 0.9 reduce-window.6
  9.0 0.2 slice_reduce_fusion
  9.2 0.1 fusion.16
  9.3 0.0 copy-start.5
  9.4 3.0 scatter_custom_fusion
  12.3 0.7 all_to_all.20
  13.0 7.3 %all-to-all-start = ((bf16[8,1,144]{2,1,0:T(2,128)(2,1)}), bf16[8,1,144]{2,1,0:T(2,128)(2,1)S(1)}, u32[]{:S(2)}, u32[]{:S(2)}) async-start(bf16[8,1,144]{2,1,0:T(2,128)(2,1)} %all_to_all.20), calls=%async_computation.1 | async-start | bytes 16384 | tf_op jit(solution)/shard_map/all_to_all | solution.py:100
  20.3 3.6 scatter_custom_fusion.2
  23.9 3.0 all-to-all-done
  26.8 3.6 all-to-all-start.2
  30.4 0.0 copy-done.5
  30.4 6.7 %scatter_custom_fusion.1 = bf16[1152,2048]{1,0:T(8,128)(2,1)} fusion(s32[384]{0:T(512)S(1)} %fusion.27, bf16[384,2048]{1,0:T(8,128)(2,1)} %param.7, bf16[]{:T(256)} %constant.166.clone.1), kind=kCustom, calls=%fused_computation.13 | custom fusion | bytes 4719104 | tf_op jit(solution)/shard_map/scatter | solution.py:67
  37.1 21.0 %all-to-all-done.2 = bf16[8,144,512]{2,1,0:T(8,128)(2,1)S(1)} async-done(((bf16[8,144,512]{2,1,0:T(8,128)(2,1)}), bf16[8,144,512]{2,1,0:T(8,128)(2,1)S(1)}, u32[]{:S(2)}, u32[]{:S(2)}) %all-to-all-start.2) | async-done | bytes 1179680 | tf_op jit(solution)/shard_map/all_to_all | solution.py:131
  58.1 4.6 %all-to-all-start.1 = ((bf16[8,144,2048]{2,1,0:T(8,128)(2,1)}), bf16[8,144,2048]{2,1,0:T(8,128)(2,1)}, u32[]{:S(2)}, u32[]{:S(2)}) async-start(bf16[8,144,2048]{2,1,0:T(8,128)(2,1)} %bitcast.74), calls=%async_computation.2 | async-start | bytes 9437184 | tf_op jit(solution)/shard_map/all_to_all | solution.py:99
  62.7 0.2 reduce-scatter.2.cloned.1.call-start
  62.9 10.0 %fusion.31 = f32[2048,384]{1,0:T(8,128)} fusion(bf16[2048,2048]{1,0:T(8,128)(2,1)} %param.8, bf16[384,2048]{1,0:T(8,128)(2,1)} %param.7), kind=kOutput, calls=%fused_computation.93 | convolution fusion | flops 3221225472 | bytes 13107200 | tf_op jit(solution)/shard_map/dot_general | solution.py:34
  72.9 0.0 reduce-scatter.2.cloned.1.call-update
  73.0 0.6 fusion.20
  73.6 0.1 eq.96
  73.7 0.0 copy-start.2
  73.7 1.5 fusion.2
  75.2 0.8 reduce_sum.48
  76.0 90.2 %all-to-all-done.1 = bf16[8,144,2048]{2,1,0:T(8,128)(2,1)} async-done(((bf16[8,144,2048]{2,1,0:T(8,128)(2,1)}), bf16[8,144,2048]{2,1,0:T(8,128)(2,1)}, u32[]{:S(2)}, u32[]{:S(2)}) %all-to-all-start.1) | async-done | bytes 4718624 | tf_op jit(solution)/shard_map/all_to_all | solution.py:99
  166.2 3.9 %convolution_select_fusion = f32[1152,256]{0,1:T(8,128)S(1)} fusion(bf16[1152,2048]{1,0:T(8,128)(2,1)} %bitcast.5, bf16[256,2048]{1,0:T(8,128)(2,1)S(1)} %bitcast.73, bf16[1152]{0:T(1024)(128)(2,1)S(1)} %eq.96, bf16[256]{0:T(256)(128)(2,1)S(1)} %fusion.28), kind=kOutput, calls=%fused_computation.12 | convolution fusion | flops 1208549376 | bytes 6949632 | tf_op jit(solution)/shard_map/dot_general | solution.py:28
  170.1 0.8 reduce_sum.47
  170.9 18.1 %all-reduce.2 = (bf16[1152,64]{0,1:T(8,128)(2,1)}, bf16[1152,64]{0,1:T(8,128)(2,1)S(1)}) all-reduce(f32[1152,64]{0,1:T(8,128)} %reduce_sum.47, f32[1152,64]{0,1:T(8,128)} %reduce_sum.48), channel_id=1, replica_groups=mesh['dp'=8,'tensor'=4] {'tensor'}, use_global_device_ids=true, to_apply=%region_8.9 | all-reduce | flops 147456 | bytes 884736 | tf_op jit(solution)/shard_map/psum | solution.py:107
  188.9 4.4 %bitcast_convert_fusion = bf16[1152,2048]{1,0:T(8,128)(2,1)} fusion(bf16[4,64,2048]{2,1,0:T(8,128)(2,1)S(1)} %copy-done, bf16[1152,64]{0,1:T(8,128)(2,1)S(1)} %get-tuple-element.21, bf16[4,64]{1,0:T(4,128)(2,1)} %fusion.20, bf16[1152]{0:T(1024)(128)(2,1)} %copy-done.2), kind=kOutput, calls=%fused_computation.5 | convolution fusion | flops 1211498496 | bytes 5917440 | tf_op jit(solution)/shard_map/dot_general | solution.py:140
  193.4 4.7 %all-to-all-start.3 = ((bf16[8,144,2048]{2,1,0:T(8,128)(2,1)}), bf16[8,144,2048]{2,1,0:T(8,128)(2,1)}, u32[]{:S(2)}, u32[]{:S(2)}) async-start(bf16[8,144,2048]{2,1,0:T(8,128)(2,1)} %bitcast.78), calls=%async_computation.4 | async-start | bytes 9437184 | tf_op jit(solution)/shard_map/all_to_all | solution.py:143
  198.1 0.0 all-gather.2.cloned.1.call-start
  198.2 0.7 all-gather.2.cloned.1.call-update
  199.1 0.6 pad_clamp_fusion
  199.8 1.7 fusion.1
  201.4 0.0 copy-done.3
  201.5 0.0 copy-done.9
  201.5 0.2 fusion.7
  201.7 1.9 collective-permute-start
  203.6 0.2 fusion.5
  203.8 5.2 %fusion.32 = f32[4,64,2048]{2,1,0:T(8,128)} fusion(bf16[4,64,1152]{2,1,0:T(8,128)(2,1)S(1)} %bitcast.84, bf16[1152,2048,1]{1,0,2:T(8,128)(2,1)} %bitcast.21), kind=kOutput, calls=%fused_computation.94 | convolution fusion | flops 1207959552 | bytes 7405568 | tf_op jit(solution)/shard_map/dot_general | solution.py:34
  209.0 73.6 %collective-permute-done = bf16[1,1,144,512]{3,2,0,1:T(8,128)(2,1)S(1)} collective-permute-done((bf16[1,1,144,512]{3,2,0,1:T(8,128)(2,1)S(1)}, bf16[1,1,144,512]{3,2,0,1:T(8,128)(2,1)S(1)}, u32[]{:S(2)}, u32[]{:S(2)}) %collective-permute-start) | collective-permute-done | bytes 147488 | tf_op jit(solution)/shard_map/ppermute | solution.py:121
  282.6 0.1 constant_dynamic-slice_fusion
  282.7 22.9 %collective-permute-start.2 = (bf16[1,1,144,512]{3,2,0,1:T(8,128)(2,1)S(1)}, bf16[1,1,144,512]{3,2,0,1:T(8,128)(2,1)S(1)}, u32[]{:S(2)}, u32[]{:S(2)}) collective-permute-start(bf16[1,1,144,512]{3,2,0,1:T(8,128)(2,1)S(1)} %get-tuple-element.26), channel_id=1, source_target_pairs={{0,12},{4,16},{8,20},{12,24},{16,28},{20,0},{24,4},{28,8},{1,13},{... | collective-permute-start | bytes 442376 | tf_op jit(solution)/shard_map/ppermute | solution.py:121
  305.6 0.0 collective-permute-start.1
  305.6 1.3 convolution_multiply_fusion.1
  306.9 6.6 %collective-permute-start.6 = (bf16[1,1,144,512]{3,2,0,1:T(8,128)(2,1)S(1)}, bf16[1,1,144,512]{3,2,0,1:T(8,128)(2,1)S(1)}, u32[]{:S(2)}, u32[]{:S(2)}) collective-permute-start(bf16[1,1,144,512]{3,2,0,1:T(8,128)(2,1)S(1)} %get-tuple-element.22), channel_id=1, source_target_pairs={{0,28},{4,0},{8,4},{12,8},{16,12},{20,16},{24,20},{28,24},{1,29},{... | collective-permute-start | bytes 442376 | tf_op jit(solution)/shard_map/ppermute | solution.py:121
  313.5 0.0 collective-permute-start.5
  313.5 0.0 collective-permute-start.4
  313.5 0.6 collective-permute-done.1
  314.1 2.3 collective-permute-start.3
  316.5 0.6 collective-permute-done.2
  317.1 14.8 %collective-permute-done.3 = bf16[1,1,144,512]{3,2,0,1:T(8,128)(2,1)S(1)} collective-permute-done((bf16[1,1,144,512]{3,2,0,1:T(8,128)(2,1)S(1)}, bf16[1,1,144,512]{3,2,0,1:T(8,128)(2,1)S(1)}, u32[]{:S(2)}, u32[]{:S(2)}) %collective-permute-start.3) | collective-permute-done | bytes 147488 | tf_op jit(solution)/shard_map/ppermute | solution.py:121
  331.8 0.0 collective-permute-done.4
  331.9 0.0 collective-permute-done.5
  331.9 0.0 collective-permute-done.6
  331.9 2.1 gather_fusion
  334.0 0.2 copy.19
  334.2 0.0 reduce-scatter.2.cloned.1.call-done
  334.3 1.2 fusion.8
  335.5 0.9 copy.20
  336.4 0.0 all-to-all-done.3
  336.4 7.3 %gather_fusion.1 = bf16[384,2048]{1,0:T(8,128)(2,1)S(1)} fusion(bf16[1152,2048]{1,0:T(8,128)(2,1)} %bitcast.17, s32[1024]{0:T(1024)S(1)} %copy-done.4), kind=kCustom, calls=%fused_computation.1 | custom fusion | bytes 3147264 | tf_op jit(solution)/shard_map/gather | solution.py:157
  343.8 0.0 all-gather.2.cloned.1.call-done
  343.8 8.5 %add_convert_fusion = bf16[384,2048]{1,0:T(8,128)(2,1)} fusion(bf16[384,2048]{1,0:T(8,128)(2,1)S(1)} %gather_fusion.1, bf16[384,2048]{1,0:T(8,128)(2,1)} %all-gather.2.cloned.1.call-done, bf16[2048,2048]{1,0:T(8,128)(2,1)} %param.8), kind=kOutput, calls=%fused_computation.8 | convolution fusion | flops 3223584768 | bytes 13107200 | tf_op jit(solution)/shard_map/dot_general | solution.py:28
  (28 shorter events, 0.3 us)
Async XLA Ops:
  7.2 159.0 %copy-start = (bf16[4,64,2048]{2,1,0:T(8,128)(2,1)S(1)}, bf16[4,64,2048]{2,1,0:T(8,128)(2,1)}, u32[]{:S(2)}) copy-start(bf16[4,64,2048]{2,1,0:T(8,128)(2,1)} %param.9) | copy-start | bytes 3145732
  9.3 21.1 %copy-start.5 = (s32[384]{0:T(512)}, s32[384]{0:T(512)S(1)}, u32[]{:S(2)}) copy-start(s32[384]{0:T(512)S(1)} %fusion.27) | copy-start | bytes 4612
  13.0 13.8 %all-to-all-start = ((bf16[8,1,144]{2,1,0:T(2,128)(2,1)}), bf16[8,1,144]{2,1,0:T(2,128)(2,1)S(1)}, u32[]{:S(2)}, u32[]{:S(2)}) async-start(bf16[8,1,144]{2,1,0:T(2,128)(2,1)} %all_to_all.20), calls=%async_computation.1 | async-start | bytes 16384 | tf_op jit(solution)/shard_map/all_to_all | solution.py:100
  26.8 31.3 %all-to-all-start.2 = ((bf16[8,144,512]{2,1,0:T(8,128)(2,1)}), bf16[8,144,512]{2,1,0:T(8,128)(2,1)S(1)}, u32[]{:S(2)}, u32[]{:S(2)}) async-start(bf16[8,144,512]{2,1,0:T(8,128)(2,1)} %bitcast.11), calls=%async_computation.3 | async-start | bytes 2359296 | tf_op jit(solution)/shard_map/all_to_all | solution.py:131
  58.1 108.1 %all-to-all-start.1 = ((bf16[8,144,2048]{2,1,0:T(8,128)(2,1)}), bf16[8,144,2048]{2,1,0:T(8,128)(2,1)}, u32[]{:S(2)}, u32[]{:S(2)}) async-start(bf16[8,144,2048]{2,1,0:T(8,128)(2,1)} %bitcast.74), calls=%async_computation.2 | async-start | bytes 9437184 | tf_op jit(solution)/shard_map/all_to_all | solution.py:99
  62.7 271.6 %reduce-scatter.2.cloned.1.call-start = ((), (), s32[]{:S(2)}) async-start(), calls=%async_computation.5 | async-start | bytes 3932160 | tf_op jit(solution)/shard_map/reduce_scatter | solution.py:159
  73.0 93.2 %copy-start.8 = (bf16[256]{0:T(256)(128)(2,1)}, bf16[256]{0:T(256)(128)(2,1)S(1)}, u32[]{:S(2)}) copy-start(bf16[256]{0:T(256)(128)(2,1)S(1)} %fusion.28) | copy-start | bytes 1540
  73.7 92.5 %copy-start.2 = (bf16[1152]{0:T(1024)(128)(2,1)}, bf16[1152]{0:T(1024)(128)(2,1)S(1)}, u32[]{:S(2)}) copy-start(bf16[1152]{0:T(1024)(128)(2,1)S(1)} %eq.96) | copy-start | bytes 6916
  193.4 5.8 %copy-start.6 = (s32[384]{0:T(512)S(1)}, s32[384]{0:T(512)}, u32[]{:S(2)}) copy-start(s32[384]{0:T(512)} %copy-done.5) | copy-start | bytes 4612
  193.4 143.0 %all-to-all-start.3 = ((bf16[8,144,2048]{2,1,0:T(8,128)(2,1)}), bf16[8,144,2048]{2,1,0:T(8,128)(2,1)}, u32[]{:S(2)}, u32[]{:S(2)}) async-start(bf16[8,144,2048]{2,1,0:T(8,128)(2,1)} %bitcast.78), calls=%async_computation.4 | async-start | bytes 9437184 | tf_op jit(solution)/shard_map/all_to_all | solution.py:143
  198.1 145.6 %all-gather.2.cloned.1.call-start = ((), (), s32[]{:S(2)}) async-start(), calls=%async_computation.6 | async-start | bytes 1966080 | tf_op jit(solution)/shard_map/all_gather | solution.py:96
  199.7 1.7 copy-start.3
  199.7 1.7 copy-start.9
  199.7 3.8 %copy-start.1 = (bf16[1152,64]{0,1:T(8,128)(2,1)S(1)}, bf16[1152,64]{0,1:T(8,128)(2,1)}, u32[]{:S(2)}) copy-start(bf16[1152,64]{0,1:T(8,128)(2,1)} %get-tuple-element.20) | copy-start | bytes 442372
  199.8 3.8 %copy-start.7 = (bf16[4,64]{1,0:T(4,128)(2,1)S(1)}, bf16[4,64]{1,0:T(4,128)(2,1)}, u32[]{:S(2)}) copy-start(bf16[4,64]{1,0:T(4,128)(2,1)} %fusion.20) | copy-start | bytes 1540
  201.7 80.9 %collective-permute-start = (bf16[1,1,144,512]{3,2,0,1:T(8,128)(2,1)S(1)}, bf16[1,1,144,512]{3,2,0,1:T(8,128)(2,1)S(1)}, u32[]{:S(2)}, u32[]{:S(2)}) collective-permute-start(bf16[1,1,144,512]{3,2,0,1:T(8,128)(2,1)S(1)} %constant_dynamic-slice_fusion.6), channel_id=1, source_target_pairs={{0,4},{4,8},{8,12},{12,16},{16,20},{20,24},{24,28},{28,0},{1,5},{5... | collective-permute-start | bytes 442376 | tf_op jit(solution)/shard_map/ppermute | solution.py:121
  282.7 34.4 %collective-permute-start.2 = (bf16[1,1,144,512]{3,2,0,1:T(8,128)(2,1)S(1)}, bf16[1,1,144,512]{3,2,0,1:T(8,128)(2,1)S(1)}, u32[]{:S(2)}, u32[]{:S(2)}) collective-permute-start(bf16[1,1,144,512]{3,2,0,1:T(8,128)(2,1)S(1)} %get-tuple-element.26), channel_id=1, source_target_pairs={{0,12},{4,16},{8,20},{12,24},{16,28},{20,0},{24,4},{28,8},{1,13},{... | collective-permute-start | bytes 442376 | tf_op jit(solution)/shard_map/ppermute | solution.py:121
  305.6 8.6 %collective-permute-start.1 = (bf16[1,1,144,512]{3,2,0,1:T(8,128)(2,1)S(1)}, bf16[1,1,144,512]{3,2,0,1:T(8,128)(2,1)S(1)}, u32[]{:S(2)}, u32[]{:S(2)}) collective-permute-start(bf16[1,1,144,512]{3,2,0,1:T(8,128)(2,1)S(1)} %get-tuple-element.27), channel_id=1, source_target_pairs={{0,8},{4,12},{8,16},{12,20},{16,24},{20,28},{24,0},{28,4},{1,9},{5... | collective-permute-start | bytes 442376 | tf_op jit(solution)/shard_map/ppermute | solution.py:121
  306.9 25.1 %copy-start.4 = (s32[1024]{0:T(1024)S(1)}, s32[1024]{0:T(1024)}, u32[]{:S(2)}) copy-start(s32[1024]{0:T(1024)} %pad_clamp_fusion) | copy-start | bytes 12292
  306.9 25.0 %collective-permute-start.6 = (bf16[1,1,144,512]{3,2,0,1:T(8,128)(2,1)S(1)}, bf16[1,1,144,512]{3,2,0,1:T(8,128)(2,1)S(1)}, u32[]{:S(2)}, u32[]{:S(2)}) collective-permute-start(bf16[1,1,144,512]{3,2,0,1:T(8,128)(2,1)S(1)} %get-tuple-element.22), channel_id=1, source_target_pairs={{0,28},{4,0},{8,4},{12,8},{16,12},{20,16},{24,20},{28,24},{1,29},{... | collective-permute-start | bytes 442376 | tf_op jit(solution)/shard_map/ppermute | solution.py:121
  313.5 18.3 %collective-permute-start.5 = (bf16[1,1,144,512]{3,2,0,1:T(8,128)(2,1)S(1)}, bf16[1,1,144,512]{3,2,0,1:T(8,128)(2,1)S(1)}, u32[]{:S(2)}, u32[]{:S(2)}) collective-permute-start(bf16[1,1,144,512]{3,2,0,1:T(8,128)(2,1)S(1)} %get-tuple-element.23), channel_id=1, source_target_pairs={{0,24},{4,28},{8,0},{12,4},{16,8},{20,12},{24,16},{28,20},{1,25},{... | collective-permute-start | bytes 442376 | tf_op jit(solution)/shard_map/ppermute | solution.py:121
  313.5 18.3 %collective-permute-start.4 = (bf16[1,1,144,512]{3,2,0,1:T(8,128)(2,1)S(1)}, bf16[1,1,144,512]{3,2,0,1:T(8,128)(2,1)S(1)}, u32[]{:S(2)}, u32[]{:S(2)}) collective-permute-start(bf16[1,1,144,512]{3,2,0,1:T(8,128)(2,1)S(1)} %get-tuple-element.24), channel_id=1, source_target_pairs={{0,20},{4,24},{8,28},{12,0},{16,4},{20,8},{24,12},{28,16},{1,21},{... | collective-permute-start | bytes 442376 | tf_op jit(solution)/shard_map/ppermute | solution.py:121
  314.1 17.7 %collective-permute-start.3 = (bf16[1,1,144,512]{3,2,0,1:T(8,128)(2,1)S(1)}, bf16[1,1,144,512]{3,2,0,1:T(8,128)(2,1)S(1)}, u32[]{:S(2)}, u32[]{:S(2)}) collective-permute-start(bf16[1,1,144,512]{3,2,0,1:T(8,128)(2,1)S(1)} %get-tuple-element.25), channel_id=1, source_target_pairs={{0,16},{4,20},{8,24},{12,28},{16,0},{20,4},{24,8},{28,12},{1,17},{... | collective-permute-start | bytes 442376 | tf_op jit(solution)/shard_map/ppermute | solution.py:121
Sparse Core Ops, SparseCore 0:
  73.1 38.9 reduce-scatter.1
  200.5 20.5 all-gather.1
